TPU v7x, 128 devices: a whole 4x4x4 slice. The times are simulated.
128 devices in a mesh: seq: 16 (over y_hi, z, core), tp: 8 (over y_lo, x).
Axes of the slice: x: 4, y: 4 (y_hi: 2, y_lo: 2; y = y_hi * 2 + y_lo), z: 4, core: 2. Of those that a mesh axis runs over, the one named last changes fastest.
Arguments:
- queries: bfloat16 [1024, 8192], P(None, 'tp'), may hold values from -80 to 80
- cache: bfloat16 [2, 16, 16384, 1024], P(None, None, 'seq', 'tp'), may hold values from -6 to 6
- draft_kv: bfloat16 [2, 1024, 1024], P(None, 'seq', 'tp'), may hold values from -9 to 9
- out_weight: bfloat16 [8192, 8192], P('tp', 'seq'), may hold values from -0.0625 to 0.0625
- lengths: int32 [16], replicated, may hold values from 1020 to 16376, as said below
- parents: int32 [16, 64], replicated, may hold values from -1 to 62, as said below
- path: int32 [16, 8], replicated, may hold values from 0 to 63, as said below
- accepted: int32 [16], replicated, may hold values from 1 to 8
Outputs:
- attn_out: bfloat16 [1024, 8192], P('tp', 'seq')
- new_cache: bfloat16 [2, 16, 16384, 1024], P(None, None, 'seq', 'tp')
Inputs may be any that keep to these rules, and one draw needn't show every extreme that they name: `lengths`: request r belongs to tenant t = r mod 4; a request of tenant t holds at most 16384 // 8 * 2 ** t - 8 tokens and at least half of that, and the first request of each tenant holds exactly that many. `parents`: node 0 is the root, with parent -1; every other node i has its parent among the nodes i - 7 to i - 1. `path`: for each request, the nodes of one branch of its tree, each the parent of the next, the last being node 63.
All inputs are finite; a program needn't handle non-finite values.
Results may differ from a plain program's by a relative error of at most 0.0051.
Values may be sent and summed in bfloat16 or wider, within the bound.
A program may use at most 192 MiB of HBM per device.

v0:
```python
import jax
import jax.numpy as jnp
from jax import lax
from jax.sharding import PartitionSpec as P

HEAD = 128
Q = 64
ACC = 8
masked_score = -1e30


def merged_2(array, axis, combine):
    everything = jax.tree.map(lambda part: lax.all_gather(part, axis), array)
    leading = jax.tree.map(lambda part: part[0], everything)

    def hop(k, so_far):
        return combine(so_far, jax.tree.map(lambda part: part[k], everything))

    return lax.fori_loop(1, lax.axis_size(axis), hop, leading)


def ancestors(parents):
    node_count = parents.shape[1]
    node_ids = jnp.arange(node_count, dtype=jnp.int32)
    step_map = (parents[:, :, None] == node_ids[None, None, :]).astype(jnp.float32)
    identity = jnp.broadcast_to(jnp.eye(node_count, dtype=jnp.float32), step_map.shape)
    reached = jnp.minimum(identity + step_map, 1.0)
    for doubling in range((node_count - 1).bit_length()):
        as_bits = reached.astype(jnp.bfloat16)
        squared = jnp.einsum("nij,njk->nik", as_bits, as_bits, preferred_element_type=jnp.float32)
        reached = jnp.minimum(squared, 1.0)
    return reached


def partial_block(query_rows, key_rows, value_rows, alive_mask):
    scores = jnp.einsum(
        "nqkge,npke->nqkgp", query_rows, key_rows, preferred_element_type=jnp.float32
    ) * HEAD ** (-0.5)
    masked = jnp.where(alive_mask, scores, masked_score)
    peak_score = jnp.max(masked, axis=-1)
    weights = jnp.where(alive_mask, jnp.exp(scores - peak_score[..., None]), 0.0)
    denominator = jnp.sum(weights, axis=-1)
    weighted = jnp.einsum(
        "nqkgp,npke->nqkge",
        weights.astype(jnp.bfloat16),
        value_rows,
        preferred_element_type=jnp.float32,
    )
    return (peak_score, denominator, weighted)


def join_flat(former, latter):
    peak_score = jnp.maximum(former[0], latter[0])
    weight_former = jnp.exp(former[0] - peak_score)
    weight_latter = jnp.exp(latter[0] - peak_score)
    row_count, head_count = peak_score.shape
    weighted = (
        former[2].reshape(row_count, head_count, -1) * weight_former[..., None]
        + latter[2].reshape(row_count, head_count, -1) * weight_latter[..., None]
    )
    return (
        peak_score,
        former[1] * weight_former + latter[1] * weight_latter,
        weighted.reshape(row_count, -1),
    )


def finish(query_flat, draft_rows, family, partials, kv_local):
    node_sets = family.shape[0]
    heads_local = query_flat.shape[1] // HEAD
    group_size = heads_local // kv_local
    reach = ancestors(family)
    query_rows = query_flat.reshape(node_sets, Q, kv_local, group_size, HEAD)
    key_rows = draft_rows[0].reshape(node_sets, Q, kv_local, HEAD)
    value_rows = draft_rows[1].reshape(node_sets, Q, kv_local, HEAD)
    draft_part = partial_block(query_rows, key_rows, value_rows, reach[:, :, None, None, :] > 0.5)
    row_count = node_sets * Q
    draft_part = (
        draft_part[0].reshape(row_count, heads_local),
        draft_part[1].reshape(row_count, heads_local),
        draft_part[2].reshape(row_count, heads_local * HEAD),
    )
    peak_score, denominator, weighted = join_flat(partials, draft_part)
    result = weighted.reshape(row_count, heads_local, HEAD) / denominator[..., None]
    return result.reshape(row_count, heads_local * HEAD).astype(jnp.bfloat16)


def select_rows(draft_rows, branch_path):
    node_sets = branch_path.shape[0]
    draft_table = draft_rows.reshape(2, node_sets, Q, draft_rows.shape[2])
    selector = (branch_path[:, :, None] == jnp.arange(Q, dtype=jnp.int32)[None, None, :]).astype(
        jnp.bfloat16
    )
    return jnp.einsum(
        "naq,xnqd->xnad", selector, draft_table, preferred_element_type=jnp.float32
    ).astype(jnp.bfloat16)


def local(queries, cache, draft_kv, out_weight, lengths, parents, path, accepted):
    seq_index = lax.axis_index("seq")
    requests = cache.shape[1]
    span_cache = cache.shape[2]
    kv_local = cache.shape[3] // HEAD
    heads_local = queries.shape[1] // HEAD
    group_size = heads_local // kv_local
    token_rows = requests * Q
    bundles = requests // 4
    positions = seq_index * span_cache + jnp.arange(span_cache, dtype=jnp.int32)
    alive_mask = positions[None, :] < lengths[:, None]
    query_blocks = queries.reshape(bundles, 4, Q, kv_local, group_size, HEAD)
    key_blocks = cache[0].reshape(bundles, 4, span_cache, kv_local, HEAD)
    value_blocks = cache[1].reshape(bundles, 4, span_cache, kv_local, HEAD)

    def cache_part(inputs):
        query_block, key_block, value_block, alive_block = inputs
        return partial_block(
            query_block, key_block, value_block, alive_block[:, None, None, None, :]
        )

    peak_score, denominator, weighted = lax.map(
        cache_part,
        (query_blocks, key_blocks, value_blocks, alive_mask.reshape(bundles, 4, span_cache)),
    )
    peak_score = peak_score.reshape(token_rows, heads_local)
    denominator = denominator.reshape(token_rows, heads_local)
    weighted = weighted.reshape(token_rows, heads_local * HEAD)
    drafts = lax.all_gather(draft_kv, "seq", axis=1, tiled=True)
    merged = merged_2((peak_score, denominator, weighted), "seq", join_flat)
    attended = finish(queries, drafts, parents, merged, kv_local)
    chosen = select_rows(drafts, path)
    attn_out = lax.psum_scatter(
        jnp.dot(attended, out_weight, preferred_element_type=jnp.float32),
        "tp",
        scatter_dimension=0,
        tiled=True,
    ).astype(jnp.bfloat16)
    offset = positions[None, :] - lengths[:, None]
    writable = (offset >= 0) & (offset < accepted[:, None])
    selector = (
        (offset[:, :, None] == jnp.arange(ACC, dtype=jnp.int32)[None, None, :])
        & writable[:, :, None]
    ).astype(jnp.bfloat16)
    placed = jnp.einsum(
        "rca,xrad->xrcd", selector, chosen, preferred_element_type=jnp.float32
    ).astype(jnp.bfloat16)
    new_cache = jnp.where(writable[None, :, :, None], placed, cache)
    return (attn_out, new_cache)


def solution(mesh):
    return jax.shard_map(
        local,
        mesh=mesh,
        in_specs=(
            P(None, "tp"),
            P(None, None, "seq", "tp"),
            P(None, "seq", "tp"),
            P("tp", "seq"),
            P(),
            P(),
            P(),
            P(),
        ),
        out_specs=(P("tp", "seq"), P(None, None, "seq", "tp")),
        check_vma=False,
    )
```

profile of v0, /device:TPU:0, one launch (start us, length us, event | category | flops | bytes accessed | tf_op | source)
XLA Modules:
  0.0 676.2 jit_solution(16713751382238479600)
XLA Ops:
  8.1 6.0 fusion.71
  14.8 38.0 %while.33 = (s32[]{:T(128)}, f32[4,4,64,1,8]{2,1,0,4,3:T(4,128)S(1)}, f32[4,4,64,1,8]{2,4,3,1,0:T(8,128)S(1)}, f32[4,4,64,1,8,128]{5,4,2,1,0,3:T(8,128)}, pred[4...) while((s32[]{:T(128)}, ...), condition=%wide.region_3.4_spmd, body=%wide.region_0.3_spmd.sunk | while | flops 1096806400 | bytes 32101996 | solution.py:120
  17.6 3.0 fusion.91
  36.6 3.0 fusion.91
  52.8 4.9 all_gather_reshape.11
  65.5 29.0 %all_gather.15 = bf16[2,1024,128]{2,1,0:T(8,128)(2,1)S(1)} all-gather(bf16[2,64,128]{2,1,0:T(8,128)(2,1)S(1)} %copy-done.7), channel_id=1, replica_groups=mesh['seq'=16,'tp'=8] {'seq'}, dimensions={1}, use_global_device_ids=true | all-gather | bytes 557056 | tf_op jit(solution)/shard_map/all_gather | solution.py:127
  103.4 23.8 %all_gather.13 = f32[16,1024,8]{1,2,0:T(8,128)S(1)} all-gather(f32[1,1024,8]{1,2,0:T(8,128)} %all_gather_reshape.10), channel_id=1, replica_groups=mesh['seq'=16,'tp'=8] {'seq'}, dimensions={0}, use_global_device_ids=true | all-gather | bytes 557056 | tf_op jit(solution)/shard_map/all_gather | solution.py:13
  127.2 22.2 %all_gather.12 = f32[16,1024,8]{1,2,0:T(8,128)S(1)} all-gather(f32[1,1024,8]{1,2,0:T(8,128)} %all_gather_reshape.9), channel_id=1, replica_groups=mesh['seq'=16,'tp'=8] {'seq'}, dimensions={0}, use_global_device_ids=true | all-gather | bytes 557056 | tf_op jit(solution)/shard_map/all_gather | solution.py:13
  149.4 4.3 fusion.73
  153.7 253.1 %all-gather.2.cloned.1.call-done = f32[16,1024,1024]{2,1,0:T(8,128)} async-done(((f32[1,1024,1024]{2,1,0:T(8,128)}), f32[16,1024,1024]{2,1,0:T(8,128)}) %all-gather.2.cloned.1.call-update) | async-done | bytes 67108880 | tf_op jit(solution)/shard_map/all_gather | solution.py:13
  406.8 4.8 slice_bitcast_fusion
  411.6 207.2 %while.34 = (s32[]{:T(128)}, f32[1024,8]{0,1:T(8,128)S(1)}, f32[1024,8]{0,1:T(8,128)S(1)}, f32[1024,1024]{1,0:T(8,128)}, f32[16,1024,8]{1,2,0:T(8,128)S(1)}, /*i...) while((s32[]{:T(128)}, f32[1024,8]{0,1:T(8,128)S(1)}, ...), condition=%wide.region_5.6_spmd, body=%wide.region_4.5_spmd.sunk | while | flops 3194885 | bytes 46596272 | solution.py:19
  416.8 8.6 %fusion.93 = f32[1024,1024]{1,0:T(8,128)} fusion(f32[128,8,8,128]{3,2,1,0:T(8,128)S(1)} %bitcast.239, f32[1024,1024]{1,0:T(8,128)} %get-tuple-element.461, f32[128,8,8,128]{3,2,1,0:T(8,128)S(1)} %bitcast.240, f32[16,1024,1024]{2,1,0:T(8,128)} %get-tuple-element.474, s32[]{:T(128)S(6)} %select_n.68), kind=kLoop, calls=%fused_computation.27.clone.1 | loop fusion | flops 3145728 | bytes 20971524 | tf_op jit(solution)/shard_map/while/body/eval_jaxpr/add | solution.py:58
  430.6 8.6 %fusion.93 = f32[1024,1024]{1,0:T(8,128)} fusion(f32[128,8,8,128]{3,2,1,0:T(8,128)S(1)} %bitcast.239, f32[1024,1024]{1,0:T(8,128)} %get-tuple-element.461, f32[128,8,8,128]{3,2,1,0:T(8,128)S(1)} %bitcast.240, f32[16,1024,1024]{2,1,0:T(8,128)} %get-tuple-element.474, s32[]{:T(128)S(6)} %select_n.68), kind=kLoop, calls=%fused_computation.27.clone.1 | loop fusion | flops 3145728 | bytes 20971524 | tf_op jit(solution)/shard_map/while/body/eval_jaxpr/add | solution.py:58
  444.4 8.6 %fusion.93 = f32[1024,1024]{1,0:T(8,128)} fusion(f32[128,8,8,128]{3,2,1,0:T(8,128)S(1)} %bitcast.239, f32[1024,1024]{1,0:T(8,128)} %get-tuple-element.461, f32[128,8,8,128]{3,2,1,0:T(8,128)S(1)} %bitcast.240, f32[16,1024,1024]{2,1,0:T(8,128)} %get-tuple-element.474, s32[]{:T(128)S(6)} %select_n.68), kind=kLoop, calls=%fused_computation.27.clone.1 | loop fusion | flops 3145728 | bytes 20971524 | tf_op jit(solution)/shard_map/while/body/eval_jaxpr/add | solution.py:58
  458.2 8.6 %fusion.93 = f32[1024,1024]{1,0:T(8,128)} fusion(f32[128,8,8,128]{3,2,1,0:T(8,128)S(1)} %bitcast.239, f32[1024,1024]{1,0:T(8,128)} %get-tuple-element.461, f32[128,8,8,128]{3,2,1,0:T(8,128)S(1)} %bitcast.240, f32[16,1024,1024]{2,1,0:T(8,128)} %get-tuple-element.474, s32[]{:T(128)S(6)} %select_n.68), kind=kLoop, calls=%fused_computation.27.clone.1 | loop fusion | flops 3145728 | bytes 20971524 | tf_op jit(solution)/shard_map/while/body/eval_jaxpr/add | solution.py:58
  472.0 8.6 %fusion.93 = f32[1024,1024]{1,0:T(8,128)} fusion(f32[128,8,8,128]{3,2,1,0:T(8,128)S(1)} %bitcast.239, f32[1024,1024]{1,0:T(8,128)} %get-tuple-element.461, f32[128,8,8,128]{3,2,1,0:T(8,128)S(1)} %bitcast.240, f32[16,1024,1024]{2,1,0:T(8,128)} %get-tuple-element.474, s32[]{:T(128)S(6)} %select_n.68), kind=kLoop, calls=%fused_computation.27.clone.1 | loop fusion | flops 3145728 | bytes 20971524 | tf_op jit(solution)/shard_map/while/body/eval_jaxpr/add | solution.py:58
  485.9 8.6 %fusion.93 = f32[1024,1024]{1,0:T(8,128)} fusion(f32[128,8,8,128]{3,2,1,0:T(8,128)S(1)} %bitcast.239, f32[1024,1024]{1,0:T(8,128)} %get-tuple-element.461, f32[128,8,8,128]{3,2,1,0:T(8,128)S(1)} %bitcast.240, f32[16,1024,1024]{2,1,0:T(8,128)} %get-tuple-element.474, s32[]{:T(128)S(6)} %select_n.68), kind=kLoop, calls=%fused_computation.27.clone.1 | loop fusion | flops 3145728 | bytes 20971524 | tf_op jit(solution)/shard_map/while/body/eval_jaxpr/add | solution.py:58
  499.7 8.6 %fusion.93 = f32[1024,1024]{1,0:T(8,128)} fusion(f32[128,8,8,128]{3,2,1,0:T(8,128)S(1)} %bitcast.239, f32[1024,1024]{1,0:T(8,128)} %get-tuple-element.461, f32[128,8,8,128]{3,2,1,0:T(8,128)S(1)} %bitcast.240, f32[16,1024,1024]{2,1,0:T(8,128)} %get-tuple-element.474, s32[]{:T(128)S(6)} %select_n.68), kind=kLoop, calls=%fused_computation.27.clone.1 | loop fusion | flops 3145728 | bytes 20971524 | tf_op jit(solution)/shard_map/while/body/eval_jaxpr/add | solution.py:58
  513.5 8.6 %fusion.93 = f32[1024,1024]{1,0:T(8,128)} fusion(f32[128,8,8,128]{3,2,1,0:T(8,128)S(1)} %bitcast.239, f32[1024,1024]{1,0:T(8,128)} %get-tuple-element.461, f32[128,8,8,128]{3,2,1,0:T(8,128)S(1)} %bitcast.240, f32[16,1024,1024]{2,1,0:T(8,128)} %get-tuple-element.474, s32[]{:T(128)S(6)} %select_n.68), kind=kLoop, calls=%fused_computation.27.clone.1 | loop fusion | flops 3145728 | bytes 20971524 | tf_op jit(solution)/shard_map/while/body/eval_jaxpr/add | solution.py:58
  527.3 8.6 %fusion.93 = f32[1024,1024]{1,0:T(8,128)} fusion(f32[128,8,8,128]{3,2,1,0:T(8,128)S(1)} %bitcast.239, f32[1024,1024]{1,0:T(8,128)} %get-tuple-element.461, f32[128,8,8,128]{3,2,1,0:T(8,128)S(1)} %bitcast.240, f32[16,1024,1024]{2,1,0:T(8,128)} %get-tuple-element.474, s32[]{:T(128)S(6)} %select_n.68), kind=kLoop, calls=%fused_computation.27.clone.1 | loop fusion | flops 3145728 | bytes 20971524 | tf_op jit(solution)/shard_map/while/body/eval_jaxpr/add | solution.py:58
  541.1 8.6 %fusion.93 = f32[1024,1024]{1,0:T(8,128)} fusion(f32[128,8,8,128]{3,2,1,0:T(8,128)S(1)} %bitcast.239, f32[1024,1024]{1,0:T(8,128)} %get-tuple-element.461, f32[128,8,8,128]{3,2,1,0:T(8,128)S(1)} %bitcast.240, f32[16,1024,1024]{2,1,0:T(8,128)} %get-tuple-element.474, s32[]{:T(128)S(6)} %select_n.68), kind=kLoop, calls=%fused_computation.27.clone.1 | loop fusion | flops 3145728 | bytes 20971524 | tf_op jit(solution)/shard_map/while/body/eval_jaxpr/add | solution.py:58
  554.9 8.6 %fusion.93 = f32[1024,1024]{1,0:T(8,128)} fusion(f32[128,8,8,128]{3,2,1,0:T(8,128)S(1)} %bitcast.239, f32[1024,1024]{1,0:T(8,128)} %get-tuple-element.461, f32[128,8,8,128]{3,2,1,0:T(8,128)S(1)} %bitcast.240, f32[16,1024,1024]{2,1,0:T(8,128)} %get-tuple-element.474, s32[]{:T(128)S(6)} %select_n.68), kind=kLoop, calls=%fused_computation.27.clone.1 | loop fusion | flops 3145728 | bytes 20971524 | tf_op jit(solution)/shard_map/while/body/eval_jaxpr/add | solution.py:58
  568.7 8.6 %fusion.93 = f32[1024,1024]{1,0:T(8,128)} fusion(f32[128,8,8,128]{3,2,1,0:T(8,128)S(1)} %bitcast.239, f32[1024,1024]{1,0:T(8,128)} %get-tuple-element.461, f32[128,8,8,128]{3,2,1,0:T(8,128)S(1)} %bitcast.240, f32[16,1024,1024]{2,1,0:T(8,128)} %get-tuple-element.474, s32[]{:T(128)S(6)} %select_n.68), kind=kLoop, calls=%fused_computation.27.clone.1 | loop fusion | flops 3145728 | bytes 20971524 | tf_op jit(solution)/shard_map/while/body/eval_jaxpr/add | solution.py:58
  582.5 8.6 %fusion.93 = f32[1024,1024]{1,0:T(8,128)} fusion(f32[128,8,8,128]{3,2,1,0:T(8,128)S(1)} %bitcast.239, f32[1024,1024]{1,0:T(8,128)} %get-tuple-element.461, f32[128,8,8,128]{3,2,1,0:T(8,128)S(1)} %bitcast.240, f32[16,1024,1024]{2,1,0:T(8,128)} %get-tuple-element.474, s32[]{:T(128)S(6)} %select_n.68), kind=kLoop, calls=%fused_computation.27.clone.1 | loop fusion | flops 3145728 | bytes 20971524 | tf_op jit(solution)/shard_map/while/body/eval_jaxpr/add | solution.py:58
  596.4 8.6 %fusion.93 = f32[1024,1024]{1,0:T(8,128)} fusion(f32[128,8,8,128]{3,2,1,0:T(8,128)S(1)} %bitcast.239, f32[1024,1024]{1,0:T(8,128)} %get-tuple-element.461, f32[128,8,8,128]{3,2,1,0:T(8,128)S(1)} %bitcast.240, f32[16,1024,1024]{2,1,0:T(8,128)} %get-tuple-element.474, s32[]{:T(128)S(6)} %select_n.68), kind=kLoop, calls=%fused_computation.27.clone.1 | loop fusion | flops 3145728 | bytes 20971524 | tf_op jit(solution)/shard_map/while/body/eval_jaxpr/add | solution.py:58
  610.2 8.6 %fusion.93 = f32[1024,1024]{1,0:T(8,128)} fusion(f32[128,8,8,128]{3,2,1,0:T(8,128)S(1)} %bitcast.239, f32[1024,1024]{1,0:T(8,128)} %get-tuple-element.461, f32[128,8,8,128]{3,2,1,0:T(8,128)S(1)} %bitcast.240, f32[16,1024,1024]{2,1,0:T(8,128)} %get-tuple-element.474, s32[]{:T(128)S(6)} %select_n.68), kind=kLoop, calls=%fused_computation.27.clone.1 | loop fusion | flops 3145728 | bytes 20971524 | tf_op jit(solution)/shard_map/while/body/eval_jaxpr/add | solution.py:58
  624.0 3.9 fusion.32
  628.0 12.3 %copy.77 = bf16[2,16,1024,128]{2,3,0,1:T(8,128)(2,1)} copy(bf16[2,16,1024,128]{3,2,1,0:T(8,128)(2,1)} %param.13) | data formatting | bytes 16777216 | tf_op args[1]
  640.5 7.2 %bitcast_select_fusion.1 = bf16[2,16,1024,128]{2,3,0,1:T(8,128)(2,1)} fusion(bf16[2,16,1024,128]{2,3,0,1:T(8,128)(2,1)} %copy.77, pred[16,1024]{1,0:T(8,128)(4,1)S(1)} %compare_and_fusion, bf16[2,16,64,128]{3,2,1,0:T(8,128)(2,1)S(1)} %bitcast.244, s32[16,1024]{1,0:T(8,128)S(1)} %broadcast_subtract_fusion, s32[16,8]{1,0:T(8,128)S(1)} %copy.75), kind=kOutput, calls=%fused_computation.35 | convolution fusion | flops 79994880 | bytes 17383936 | tf_op jit(solution)/shard_map/rca,xrad->xrcd/dot_general | solution.py:143
  647.7 11.9 %copy.78 = bf16[2,16,1024,128]{3,2,1,0:T(8,128)(2,1)} copy(bf16[2,16,1024,128]{2,3,0,1:T(8,128)(2,1)} %bitcast_select_fusion.1) | data formatting | bytes 16777216
  659.6 8.2 %reduce-scatter.2.cloned.1.call-done = f32[128,512]{1,0:T(8,128)} async-done(((f32[1024,512]{1,0:T(8,128)}), f32[128,512]{1,0:T(8,128)}) %reduce-scatter.2.cloned.1.call-update) | async-done | bytes 262160 | tf_op jit(solution)/shard_map/reduce_scatter | solution.py:131
  (197 shorter events, 134.6 us)
Async XLA Ops:
  7.2 615.7 %copy-start = (bf16[1024,512]{1,0:T(8,128)(2,1)S(1)}, bf16[1024,512]{1,0:T(8,128)(2,1)}, u32[]{:S(2)}) copy-start(bf16[1024,512]{1,0:T(8,128)(2,1)} %param.15) | copy-start | bytes 3145732
  7.2 399.6 %all-gather.2.cloned.1.call-start = ((), (), s32[]{:S(2)}) async-start(), calls=%async_computation.1 | async-start | bytes 71303168 | tf_op jit(solution)/shard_map/all_gather | solution.py:13
  8.1 6.0 copy-start.6
  57.7 1.6 copy-start.11
  57.7 7.8 %copy-start.7 = (bf16[2,64,128]{2,1,0:T(8,128)(2,1)S(1)}, bf16[2,64,128]{2,1,0:T(8,128)(2,1)}, u32[]{:S(2)}) copy-start(bf16[2,64,128]{2,1,0:T(8,128)(2,1)} %param.14) | copy-start | bytes 98308
  57.7 610.0 %reduce-scatter.2.cloned.1.call-start = ((), (), s32[]{:S(2)}) async-start(), calls=%async_computation.2 | async-start | bytes 2359296 | tf_op jit(solution)/shard_map/reduce_scatter | solution.py:131
  94.5 0.8 copy-start.3
  414.6 2.2 copy-start.1
  428.4 2.2 copy-start.1
  442.2 2.2 copy-start.1
  456.0 2.2 copy-start.1
  469.9 2.2 copy-start.1
  483.7 2.2 copy-start.1
  497.5 2.2 copy-start.1
  511.3 2.2 copy-start.1
  525.1 2.2 copy-start.1
  538.9 2.2 copy-start.1
  552.7 2.2 copy-start.1
  566.5 2.2 copy-start.1
  580.4 2.2 copy-start.1
  594.2 2.2 copy-start.1
  608.0 2.2 copy-start.1
  620.6 2.3 copy-start.2
  620.6 3.5 copy-start.5
  627.9 12.4 %copy-start.9 = (s32[16,8]{0,1:T(8,128)S(1)}, s32[16,8]{0,1:T(8,128)}, u32[]{:S(2)}) copy-start(s32[16,8]{0,1:T(8,128)} %param.18) | copy-start | bytes 1540
  628.0 12.4 %copy-start.8 = (s32[16]{0:T(128)S(1)}, s32[16]{0:T(128)}, u32[]{:S(2)}) copy-start(s32[16]{0:T(128)} %param.16) | copy-start | bytes 196
  628.0 12.4 %copy-start.10 = (s32[16]{0:T(128)S(1)}, s32[16]{0:T(128)}, u32[]{:S(2)}) copy-start(s32[16]{0:T(128)} %param.19) | copy-start | bytes 196
  628.0 12.6 %copy-start.4 = (bf16[2,1024,128]{2,1,0:T(8,128)(2,1)S(1)}, bf16[2,1024,128]{2,1,0:T(8,128)(2,1)}, u32[]{:S(2)}) copy-start(bf16[2,1024,128]{2,1,0:T(8,128)(2,1)} %copy-done.3) | copy-start | bytes 1572868
Sparse Core Ops, SparseCore 0:
  57.8 348.9 all-gather.1
  628.1 39.6 reduce-scatter.1
where the time goes:
time: 678 us; the launch traced here: 676 us
  waiting for transfers between devices  261 us (38%)
  other arithmetic  141 us (21%)
  local copies, waits for them, and re-layouts  137 us (20%)
  blocking collectives  74.9 us (11%)
  matrix products  46.3 us (7%)
  between operations  14.3 us (2%)
    all_gather x1, waiting for transfers between devices, merged_2(): everything = jax.tree.map(lambda part: lax.all_gather(part, axis), array)  253 us
    add x15, other arithmetic, join_flat(): former[2].reshape(row_count, head_count, -1) * weight_former[..., None]  129 us
    all_gather x2, blocking collectives, merged_2(): everything = jax.tree.map(lambda part: lax.all_gather(part, axis), array)  46 us
    mul x16, local copies, waits for them, and re-layouts, join_flat(): latter[2].reshape(row_count, head_count, -1) * weight_latter[..., None]  39.8 us
    all_gather x1, blocking collectives, local(): drafts = lax.all_gather(draft_kv, 'seq', axis=1, tiled=True)  29 us
    unnamed x26, local copies, waits for them, and re-layouts  26.8 us
    mul x16, local copies, waits for them, and re-layouts, join_flat(): former[2].reshape(row_count, head_count, -1) * weight_former[..., None]  18.2 us
    dot_general x5, matrix products, partial_block(): jnp.einsum('nqkgp,npke->nqkge', weights.astype(jnp.bfloat16), value_rows,...  16.4 us
  transfers between devices with their start and end apart: 2, of which 2 were waited for; matrix products, arithmetic and copies ran while one was open for 8% of the time, Pallas kernels for 0%

commit v1 on v0

--- a/solution.py
+++ b/solution.py
@@ -1,3 +1,4 @@
+import functools
 import jax
 import jax.numpy as jnp
 from jax import lax
@@ -7,6 +8,16 @@
 Q = 64
 ACC = 8
 masked_score = -1e30
+
+
+def _list_side(sample, across):
+    x_next = jnp.concatenate(
+        lax.all_to_all(jnp.stack([sample] * lax.axis_size(across), axis=0), across, 0, 0), axis=1
+    )
+    return x_next
+
+
+supply_all_panels = functools.partial(_list_side, across="seq")
 
 
 def merged_2(array, axis, combine):
@@ -124,7 +135,7 @@
     peak_score = peak_score.reshape(token_rows, heads_local)
     denominator = denominator.reshape(token_rows, heads_local)
     weighted = weighted.reshape(token_rows, heads_local * HEAD)
-    drafts = lax.all_gather(draft_kv, "seq", axis=1, tiled=True)
+    drafts = supply_all_panels(draft_kv)
     merged = merged_2((peak_score, denominator, weighted), "seq", join_flat)
     attended = finish(queries, drafts, parents, merged, kv_local)
     chosen = select_rows(drafts, path)

time: 678 us -> 690 us (1.018)
  blocking collectives: 74.9 us -> 52.4 us
  other arithmetic: 141 us -> 153 us
  waiting for transfers between devices: 261 us -> 273 us
  starting transfers between devices: 0.08 us -> 8.25 us
    all_gather x1 -> x0, blocking collectives: 29 us -> none  [local(): drafts = lax.all_gather(draft_kv, 'seq', axis=1, tiled=True)]
    all_gather x1, waiting for transfers between devices: 253 us -> 265 us  [merged_2(): everything = jax.tree.map(lambda part: lax.all_gather(part, axis), array)]
    add x16, other arithmetic: 0.4 us -> 12.2 us  [join_flat(): former[1] * weight_former + latter[1] * weight_latter]
    all_to_all x0 -> x1, starting transfers between devices: none -> 8.18 us  [_list_side(): lax.all_to_all(jnp.stack([sample] * lax.axis_size(across), axis=0), acros...]
    unnamed x26 -> x28, local copies, waits for them, and re-layouts: 26.8 us -> 28.3 us
  transfers between devices with their start and end apart: 2 -> 3, of which waited for: 2 -> 2; matrix products, arithmetic and copies ran while one was open for 8% -> 7% of each run, Pallas kernels for 0% -> 0%
where the time goes in v1:
time: 690 us; the launch traced here: 687 us
  waiting for transfers between devices  273 us (40%)
  other arithmetic  153 us (22%)
  local copies, waits for them, and re-layouts  139 us (20%)
  blocking collectives  52.4 us (8%)
  matrix products  46.6 us (7%)
  between operations  14.3 us (2%)
  starting transfers between devices  8.25 us (1%)
    all_gather x1, waiting for transfers between devices, merged_2(): everything = jax.tree.map(lambda part: lax.all_gather(part, axis), array)  265 us
    add x15, other arithmetic, join_flat(): former[2].reshape(row_count, head_count, -1) * weight_former[..., None]  129 us
    all_gather x2, blocking collectives, merged_2(): everything = jax.tree.map(lambda part: lax.all_gather(part, axis), array)  52.4 us
    mul x16, local copies, waits for them, and re-layouts, join_flat(): latter[2].reshape(row_count, head_count, -1) * weight_latter[..., None]  40.3 us
    unnamed x28, local copies, waits for them, and re-layouts  28.3 us
    mul x16, local copies, waits for them, and re-layouts, join_flat(): former[2].reshape(row_count, head_count, -1) * weight_former[..., None]  18.2 us
    dot_general x5, matrix products, partial_block(): jnp.einsum('nqkgp,npke->nqkge', weights.astype(jnp.bfloat16), value_rows,...  16.4 us
    while x30, local copies, waits for them, and re-layouts  15.7 us
  transfers between devices with their start and end apart: 3, of which 2 were waited for; matrix products, arithmetic and copies ran while one was open for 7% of the time, Pallas kernels for 0%

profile of v1, /device:TPU:0, one launch (start us, length us, event | category | flops | bytes accessed | tf_op | source)
XLA Modules:
  0.0 687.4 jit_solution(9212866516709958332)
XLA Ops:
  8.1 6.0 fusion.72
  14.8 38.0 %while.33 = (s32[]{:T(128)}, f32[4,4,64,1,8]{2,1,0,4,3:T(4,128)S(1)}, f32[4,4,64,1,8]{2,4,3,1,0:T(8,128)S(1)}, f32[4,4,64,1,8,128]{5,4,2,1,0,3:T(8,128)}, pred[4...) while((s32[]{:T(128)}, ...), condition=%wide.region_3.4_spmd, body=%wide.region_0.3_spmd.sunk | while | flops 1096806400 | bytes 32101996 | solution.py:131
  27.1 3.0 fusion.88
  46.1 3.0 fusion.88
  52.8 4.9 all_gather_reshape.11
  59.4 8.2 %all-to-all-start = ((bf16[16,2,64,128]{3,2,1,0:T(8,128)(2,1)}), bf16[16,2,64,128]{3,2,1,0:T(8,128)(2,1)}, u32[]{:S(2)}, u32[]{:S(2)}) async-start(bf16[16,2,64,128]{3,2,1,0:T(8,128)(2,1)} %stack.2), calls=%async_computation | async-start | bytes 1048576 | tf_op jit(solution)/shard_map/all_to_all | solution.py:15
  73.8 28.8 %all_gather.10 = f32[16,1024,8]{1,2,0:T(8,128)S(1)} all-gather(f32[1,1024,8]{1,2,0:T(8,128)S(1)} %all_gather_reshape.10), channel_id=1, replica_groups=mesh['seq'=16,'tp'=8] {'seq'}, dimensions={0}, use_global_device_ids=true | all-gather | bytes 557056 | tf_op jit(solution)/shard_map/all_gather | solution.py:24
  103.8 23.6 %all_gather.9 = f32[16,1024,8]{1,2,0:T(8,128)S(1)} all-gather(f32[1,1024,8]{1,2,0:T(8,128)S(1)} %all_gather_reshape.9), channel_id=1, replica_groups=mesh['seq'=16,'tp'=8] {'seq'}, dimensions={0}, use_global_device_ids=true | all-gather | bytes 557056 | tf_op jit(solution)/shard_map/all_gather | solution.py:24
  136.2 4.3 fusion.46
  140.4 265.3 %all-gather.2.cloned.1.call-done = f32[16,1024,1024]{2,1,0:T(8,128)} async-done(((f32[1,1024,1024]{2,1,0:T(8,128)}), f32[16,1024,1024]{2,1,0:T(8,128)}) %all-gather.2.cloned.1.call-update) | async-done | bytes 67108880 | tf_op jit(solution)/shard_map/all_gather | solution.py:24
  405.8 4.8 slice_bitcast_fusion
  410.6 219.5 %while.34 = (s32[]{:T(128)}, f32[1024,8]{0,1:T(8,128)S(1)}, f32[1024,8]{0,1:T(8,128)S(1)}, f32[1024,1024]{1,0:T(8,128)}, f32[16,1024,8]{1,2,0:T(8,128)}, /*index...) while((s32[]{:T(128)}, f32[1024,8]{0,1:T(8,128)S(1)}, ...), condition=%wide.region_5.6_spmd, body=%wide.region_4.5_spmd.sunk | while | flops 3194885 | bytes 46596272 | solution.py:30
  416.6 8.6 %fusion.90 = f32[1024,1024]{1,0:T(8,128)} fusion(f32[128,8,8,128]{3,2,1,0:T(8,128)S(1)} %bitcast.247, f32[1024,1024]{1,0:T(8,128)} %get-tuple-element.459, f32[128,8,8,128]{3,2,1,0:T(8,128)S(1)} %bitcast.248, f32[16,1024,1024]{2,1,0:T(8,128)} %get-tuple-element.472, s32[]{:T(128)S(6)} %select_n.68), kind=kLoop, calls=%fused_computation.27.clone.1 | loop fusion | flops 3145728 | bytes 20971524 | tf_op jit(solution)/shard_map/while/body/eval_jaxpr/add | solution.py:69
  431.2 8.6 %fusion.90 = f32[1024,1024]{1,0:T(8,128)} fusion(f32[128,8,8,128]{3,2,1,0:T(8,128)S(1)} %bitcast.247, f32[1024,1024]{1,0:T(8,128)} %get-tuple-element.459, f32[128,8,8,128]{3,2,1,0:T(8,128)S(1)} %bitcast.248, f32[16,1024,1024]{2,1,0:T(8,128)} %get-tuple-element.472, s32[]{:T(128)S(6)} %select_n.68), kind=kLoop, calls=%fused_computation.27.clone.1 | loop fusion | flops 3145728 | bytes 20971524 | tf_op jit(solution)/shard_map/while/body/eval_jaxpr/add | solution.py:69
  445.9 8.6 %fusion.90 = f32[1024,1024]{1,0:T(8,128)} fusion(f32[128,8,8,128]{3,2,1,0:T(8,128)S(1)} %bitcast.247, f32[1024,1024]{1,0:T(8,128)} %get-tuple-element.459, f32[128,8,8,128]{3,2,1,0:T(8,128)S(1)} %bitcast.248, f32[16,1024,1024]{2,1,0:T(8,128)} %get-tuple-element.472, s32[]{:T(128)S(6)} %select_n.68), kind=kLoop, calls=%fused_computation.27.clone.1 | loop fusion | flops 3145728 | bytes 20971524 | tf_op jit(solution)/shard_map/while/body/eval_jaxpr/add | solution.py:69
  460.5 8.6 %fusion.90 = f32[1024,1024]{1,0:T(8,128)} fusion(f32[128,8,8,128]{3,2,1,0:T(8,128)S(1)} %bitcast.247, f32[1024,1024]{1,0:T(8,128)} %get-tuple-element.459, f32[128,8,8,128]{3,2,1,0:T(8,128)S(1)} %bitcast.248, f32[16,1024,1024]{2,1,0:T(8,128)} %get-tuple-element.472, s32[]{:T(128)S(6)} %select_n.68), kind=kLoop, calls=%fused_computation.27.clone.1 | loop fusion | flops 3145728 | bytes 20971524 | tf_op jit(solution)/shard_map/while/body/eval_jaxpr/add | solution.py:69
  475.1 8.6 %fusion.90 = f32[1024,1024]{1,0:T(8,128)} fusion(f32[128,8,8,128]{3,2,1,0:T(8,128)S(1)} %bitcast.247, f32[1024,1024]{1,0:T(8,128)} %get-tuple-element.459, f32[128,8,8,128]{3,2,1,0:T(8,128)S(1)} %bitcast.248, f32[16,1024,1024]{2,1,0:T(8,128)} %get-tuple-element.472, s32[]{:T(128)S(6)} %select_n.68), kind=kLoop, calls=%fused_computation.27.clone.1 | loop fusion | flops 3145728 | bytes 20971524 | tf_op jit(solution)/shard_map/while/body/eval_jaxpr/add | solution.py:69
  489.8 8.6 %fusion.90 = f32[1024,1024]{1,0:T(8,128)} fusion(f32[128,8,8,128]{3,2,1,0:T(8,128)S(1)} %bitcast.247, f32[1024,1024]{1,0:T(8,128)} %get-tuple-element.459, f32[128,8,8,128]{3,2,1,0:T(8,128)S(1)} %bitcast.248, f32[16,1024,1024]{2,1,0:T(8,128)} %get-tuple-element.472, s32[]{:T(128)S(6)} %select_n.68), kind=kLoop, calls=%fused_computation.27.clone.1 | loop fusion | flops 3145728 | bytes 20971524 | tf_op jit(solution)/shard_map/while/body/eval_jaxpr/add | solution.py:69
  504.4 8.6 %fusion.90 = f32[1024,1024]{1,0:T(8,128)} fusion(f32[128,8,8,128]{3,2,1,0:T(8,128)S(1)} %bitcast.247, f32[1024,1024]{1,0:T(8,128)} %get-tuple-element.459, f32[128,8,8,128]{3,2,1,0:T(8,128)S(1)} %bitcast.248, f32[16,1024,1024]{2,1,0:T(8,128)} %get-tuple-element.472, s32[]{:T(128)S(6)} %select_n.68), kind=kLoop, calls=%fused_computation.27.clone.1 | loop fusion | flops 3145728 | bytes 20971524 | tf_op jit(solution)/shard_map/while/body/eval_jaxpr/add | solution.py:69
  519.0 8.6 %fusion.90 = f32[1024,1024]{1,0:T(8,128)} fusion(f32[128,8,8,128]{3,2,1,0:T(8,128)S(1)} %bitcast.247, f32[1024,1024]{1,0:T(8,128)} %get-tuple-element.459, f32[128,8,8,128]{3,2,1,0:T(8,128)S(1)} %bitcast.248, f32[16,1024,1024]{2,1,0:T(8,128)} %get-tuple-element.472, s32[]{:T(128)S(6)} %select_n.68), kind=kLoop, calls=%fused_computation.27.clone.1 | loop fusion | flops 3145728 | bytes 20971524 | tf_op jit(solution)/shard_map/while/body/eval_jaxpr/add | solution.py:69
  533.7 8.6 %fusion.90 = f32[1024,1024]{1,0:T(8,128)} fusion(f32[128,8,8,128]{3,2,1,0:T(8,128)S(1)} %bitcast.247, f32[1024,1024]{1,0:T(8,128)} %get-tuple-element.459, f32[128,8,8,128]{3,2,1,0:T(8,128)S(1)} %bitcast.248, f32[16,1024,1024]{2,1,0:T(8,128)} %get-tuple-element.472, s32[]{:T(128)S(6)} %select_n.68), kind=kLoop, calls=%fused_computation.27.clone.1 | loop fusion | flops 3145728 | bytes 20971524 | tf_op jit(solution)/shard_map/while/body/eval_jaxpr/add | solution.py:69
  548.3 8.6 %fusion.90 = f32[1024,1024]{1,0:T(8,128)} fusion(f32[128,8,8,128]{3,2,1,0:T(8,128)S(1)} %bitcast.247, f32[1024,1024]{1,0:T(8,128)} %get-tuple-element.459, f32[128,8,8,128]{3,2,1,0:T(8,128)S(1)} %bitcast.248, f32[16,1024,1024]{2,1,0:T(8,128)} %get-tuple-element.472, s32[]{:T(128)S(6)} %select_n.68), kind=kLoop, calls=%fused_computation.27.clone.1 | loop fusion | flops 3145728 | bytes 20971524 | tf_op jit(solution)/shard_map/while/body/eval_jaxpr/add | solution.py:69
  562.9 8.6 %fusion.90 = f32[1024,1024]{1,0:T(8,128)} fusion(f32[128,8,8,128]{3,2,1,0:T(8,128)S(1)} %bitcast.247, f32[1024,1024]{1,0:T(8,128)} %get-tuple-element.459, f32[128,8,8,128]{3,2,1,0:T(8,128)S(1)} %bitcast.248, f32[16,1024,1024]{2,1,0:T(8,128)} %get-tuple-element.472, s32[]{:T(128)S(6)} %select_n.68), kind=kLoop, calls=%fused_computation.27.clone.1 | loop fusion | flops 3145728 | bytes 20971524 | tf_op jit(solution)/shard_map/while/body/eval_jaxpr/add | solution.py:69
  577.6 8.6 %fusion.90 = f32[1024,1024]{1,0:T(8,128)} fusion(f32[128,8,8,128]{3,2,1,0:T(8,128)S(1)} %bitcast.247, f32[1024,1024]{1,0:T(8,128)} %get-tuple-element.459, f32[128,8,8,128]{3,2,1,0:T(8,128)S(1)} %bitcast.248, f32[16,1024,1024]{2,1,0:T(8,128)} %get-tuple-element.472, s32[]{:T(128)S(6)} %select_n.68), kind=kLoop, calls=%fused_computation.27.clone.1 | loop fusion | flops 3145728 | bytes 20971524 | tf_op jit(solution)/shard_map/while/body/eval_jaxpr/add | solution.py:69
  592.2 8.6 %fusion.90 = f32[1024,1024]{1,0:T(8,128)} fusion(f32[128,8,8,128]{3,2,1,0:T(8,128)S(1)} %bitcast.247, f32[1024,1024]{1,0:T(8,128)} %get-tuple-element.459, f32[128,8,8,128]{3,2,1,0:T(8,128)S(1)} %bitcast.248, f32[16,1024,1024]{2,1,0:T(8,128)} %get-tuple-element.472, s32[]{:T(128)S(6)} %select_n.68), kind=kLoop, calls=%fused_computation.27.clone.1 | loop fusion | flops 3145728 | bytes 20971524 | tf_op jit(solution)/shard_map/while/body/eval_jaxpr/add | solution.py:69
  606.8 8.6 %fusion.90 = f32[1024,1024]{1,0:T(8,128)} fusion(f32[128,8,8,128]{3,2,1,0:T(8,128)S(1)} %bitcast.247, f32[1024,1024]{1,0:T(8,128)} %get-tuple-element.459, f32[128,8,8,128]{3,2,1,0:T(8,128)S(1)} %bitcast.248, f32[16,1024,1024]{2,1,0:T(8,128)} %get-tuple-element.472, s32[]{:T(128)S(6)} %select_n.68), kind=kLoop, calls=%fused_computation.27.clone.1 | loop fusion | flops 3145728 | bytes 20971524 | tf_op jit(solution)/shard_map/while/body/eval_jaxpr/add | solution.py:69
  621.5 8.6 %fusion.90 = f32[1024,1024]{1,0:T(8,128)} fusion(f32[128,8,8,128]{3,2,1,0:T(8,128)S(1)} %bitcast.247, f32[1024,1024]{1,0:T(8,128)} %get-tuple-element.459, f32[128,8,8,128]{3,2,1,0:T(8,128)S(1)} %bitcast.248, f32[16,1024,1024]{2,1,0:T(8,128)} %get-tuple-element.472, s32[]{:T(128)S(6)} %select_n.68), kind=kLoop, calls=%fused_computation.27.clone.1 | loop fusion | flops 3145728 | bytes 20971524 | tf_op jit(solution)/shard_map/while/body/eval_jaxpr/add | solution.py:69
  635.3 3.9 fusion.32
  639.3 12.3 %copy.80 = bf16[2,16,1024,128]{2,3,0,1:T(8,128)(2,1)} copy(bf16[2,16,1024,128]{3,2,1,0:T(8,128)(2,1)} %param.13) | data formatting | bytes 16777216 | tf_op args[1]
  651.8 7.4 %bitcast_select_fusion.1 = bf16[2,16,1024,128]{2,3,0,1:T(8,128)(2,1)} fusion(bf16[2,16,1024,128]{2,3,0,1:T(8,128)(2,1)} %copy.80, pred[16,1024]{1,0:T(8,128)(4,1)S(1)} %compare_and_fusion, bf16[16,2,64,128]{3,2,1,0:T(8,128)(2,1)} %all-to-all-done, s32[16,1024]{1,0:T(8,128)S(1)} %broadcast_subtract_fusion, s32[16,8]{1,0:T(8,128)S(1)} %copy.78), kind=kOutput, calls=%fused_computation.35 | convolution fusion | flops 79994880 | bytes 17383936 | tf_op jit(solution)/shard_map/rca,xrad->xrcd/dot_general | solution.py:154
  659.2 11.9 %copy.81 = bf16[2,16,1024,128]{3,2,1,0:T(8,128)(2,1)} copy(bf16[2,16,1024,128]{2,3,0,1:T(8,128)(2,1)} %bitcast_select_fusion.1) | data formatting | bytes 16777216
  671.0 7.9 %reduce-scatter.2.cloned.1.call-done = f32[128,512]{1,0:T(8,128)} async-done(((f32[1024,512]{1,0:T(8,128)}), f32[128,512]{1,0:T(8,128)}) %reduce-scatter.2.cloned.1.call-update) | async-done | bytes 262160 | tf_op jit(solution)/shard_map/reduce_scatter | solution.py:142
  (201 shorter events, 148.0 us)
Async XLA Ops:
  7.2 627.0 %copy-start = (bf16[1024,512]{1,0:T(8,128)(2,1)S(1)}, bf16[1024,512]{1,0:T(8,128)(2,1)}, u32[]{:S(2)}) copy-start(bf16[1024,512]{1,0:T(8,128)(2,1)} %param.15) | copy-start | bytes 3145732
  7.2 398.6 %all-gather.2.cloned.1.call-start = ((), (), s32[]{:S(2)}) async-start(), calls=%async_computation.2 | async-start | bytes 71303168 | tf_op jit(solution)/shard_map/all_gather | solution.py:24
  8.1 6.0 copy-start.5
  57.7 0.8 copy-start.8
  57.7 10.1 %copy-start.12 = (s32[16,64]{1,0:T(8,128)S(1)}, s32[16,64]{1,0:T(8,128)}, u32[]{:S(2)}) copy-start(s32[16,64]{1,0:T(8,128)} %param.17) | copy-start | bytes 12292
  59.4 68.8 %all-to-all-start = ((bf16[16,2,64,128]{3,2,1,0:T(8,128)(2,1)}), bf16[16,2,64,128]{3,2,1,0:T(8,128)(2,1)}, u32[]{:S(2)}, u32[]{:S(2)}) async-start(bf16[16,2,64,128]{3,2,1,0:T(8,128)(2,1)} %stack.2), calls=%async_computation | async-start | bytes 1048576 | tf_op jit(solution)/shard_map/all_to_all | solution.py:15
  67.6 611.4 %reduce-scatter.2.cloned.1.call-start = ((), (), s32[]{:S(2)}) async-start(), calls=%async_computation.3 | async-start | bytes 2359296 | tf_op jit(solution)/shard_map/reduce_scatter | solution.py:142
  102.6 0.8 copy-start.6
  127.4 0.8 copy-start.7
  129.3 2.2 copy-start.4
  414.4 2.2 copy-start.1
  429.0 2.2 copy-start.1
  443.7 2.2 copy-start.1
  458.3 2.2 copy-start.1
  472.9 2.2 copy-start.1
  487.6 2.2 copy-start.1
  502.2 2.2 copy-start.1
  516.8 2.2 copy-start.1
  531.5 2.2 copy-start.1
  546.1 2.2 copy-start.1
  560.7 2.2 copy-start.1
  575.4 2.2 copy-start.1
  590.0 2.2 copy-start.1
  604.6 2.2 copy-start.1
  619.3 2.2 copy-start.1
  631.9 2.3 copy-start.2
  631.9 3.5 copy-start.3
  639.2 12.3 %copy-start.10 = (s32[16,8]{0,1:T(8,128)S(1)}, s32[16,8]{0,1:T(8,128)}, u32[]{:S(2)}) copy-start(s32[16,8]{0,1:T(8,128)} %param.18) | copy-start | bytes 1540
  639.2 12.4 %copy-start.9 = (s32[16]{0:T(128)S(1)}, s32[16]{0:T(128)}, u32[]{:S(2)}) copy-start(s32[16]{0:T(128)} %param.16) | copy-start | bytes 196
  639.3 12.3 %copy-start.11 = (s32[16]{0:T(128)S(1)}, s32[16]{0:T(128)}, u32[]{:S(2)}) copy-start(s32[16]{0:T(128)} %param.19) | copy-start | bytes 196
Sparse Core Ops, SparseCore 0:
  57.9 347.8 all-gather.1
  639.4 39.5 reduce-scatter.1
